TPU v7x, 512 devices: a whole 4x8x8 slice. The times are simulated.
512 devices in a mesh: doc: 32 (over y, x), seq: 16 (over z, core).
Axes of the slice: x: 4, y: 8, z: 8, core: 2. Of those that a mesh axis runs over, the one named last changes fastest.
Arguments:
- tokens: bfloat16 [131072, 1024], P(('doc', 'seq')), parts along dimension 0, may hold values from -8 to 8
- bottom_qkv: bfloat16 [1024, 3072], P('seq'), may hold values from -1 to 1
- bottom_out: bfloat16 [1024, 1024], P('seq'), may hold values from -0.5 to 0.5
- top_qkv: bfloat16 [1024, 3, 1024], P(None, None, 'seq'), may hold values from -1 to 1
- top_out: bfloat16 [1024, 1024], P('seq'), may hold values from -0.5 to 0.5
- cross_query: bfloat16 [1024, 1024], P('seq'), may hold values from -1 to 1
- cross_kv: bfloat16 [1024, 2, 1024], P(None, None, 'seq'), may hold values from -1 to 1
- cross_out: bfloat16 [1024, 1024], P('seq'), may hold values from -0.5 to 0.5
Outputs:
- encoded: bfloat16 [131072, 1024], P(('doc', 'seq')), parts along dimension 0
There are 32 independent parts, one for each index of `doc`. A program takes and returns all parts, laid end to end along the dimension named above; an argument that names none is the same for every part. Nothing has to cross between parts.
All inputs are finite; a program needn't handle non-finite values.
Results may differ from a plain program's by a relative error of at most 0.013.
Values may be sent and summed in bfloat16 or wider, within the bound.
A program may use at most 64 MiB of HBM per device.

v0:
```python
import math

import jax
import jax.numpy as jnp
from jax import lax
from jax.sharding import PartitionSpec as P

H = 16
W = 512
POOL = 32


EPS = 1e-06


def padded(cells, sides, width):
    for axis, dim in sides:
        count = lax.axis_size(axis)
        ends = count - 1
        head = lax.slice_in_dim(cells, 0, width, axis=dim)
        tail = lax.slice_in_dim(cells, cells.shape[dim] - width, cells.shape[dim], axis=dim)
        cells = jnp.concatenate(
            [
                lax.ppermute(tail, axis, [(i, (i + 1) % count) for i in range(ends)]),
                cells,
                lax.ppermute(head, axis, [((i + 1) % count, i) for i in range(ends)]),
            ],
            axis=dim,
        )
    return cells


def normed(values_in):
    values_in = values_in.astype(jnp.float32)
    return (
        values_in * lax.rsqrt(jnp.mean(values_in * values_in, axis=-1, keepdims=True) + EPS)
    ).astype(jnp.bfloat16)


def window_mask(first_tok, tok_count, half_win, total_tok):
    query_pos = first_tok + jnp.arange(tok_count, dtype=jnp.int32)
    key_pos = first_tok - half_win + jnp.arange(tok_count + 2 * half_win, dtype=jnp.int32)
    offsets = key_pos[None, :] - query_pos[:, None]
    inside = (key_pos[None, :] >= 0) & (key_pos[None, :] < total_tok)
    return (offsets >= -half_win) & (offsets < half_win) & inside


def attend(queries, key_mat, value_mat, allowed, head_count):
    row_count = queries.shape[0]
    key_count = key_mat.shape[0]
    head_width = queries.shape[1] // head_count
    score_scale = 1.0 / math.sqrt(head_width)
    split_q = queries.reshape(row_count, head_count, head_width).transpose(1, 0, 2)
    split_k = key_mat.reshape(key_count, head_count, head_width).transpose(1, 0, 2)
    split_v = value_mat.reshape(key_count, head_count, head_width).transpose(1, 0, 2)

    def one_head(operands):
        query_h, key_h, value_h = operands
        scores = jnp.dot(query_h, key_h.T, preferred_element_type=jnp.float32) * score_scale
        if allowed is not None:
            scores = jnp.where(allowed, scores, -1e30)
        row_peak = jnp.max(scores, axis=1, keepdims=True)
        expo = jnp.exp(scores - row_peak)
        row_total = jnp.sum(expo, axis=1, keepdims=True)
        mixture = (
            jnp.dot(expo.astype(jnp.bfloat16), value_h, preferred_element_type=jnp.float32)
            / row_total
        )
        return mixture.astype(jnp.bfloat16)

    merged = lax.map(one_head, (split_q, split_k, split_v))
    return merged.transpose(1, 0, 2).reshape(row_count, head_count * head_width)


def fold_rows(operand, shard_rows):
    return jnp.dot(operand, shard_rows, preferred_element_type=jnp.float32)


def local(tokens, bottom_qkv, bottom_out, top_qkv, top_out, cross_query, cross_kv, cross_out):
    tok_count, model_width = tokens.shape
    devices_seq = lax.axis_size("seq")
    local_heads = H // devices_seq
    half_win = W // 2
    total_tok = tok_count * devices_seq
    first_tok = lax.axis_index("seq") * tok_count
    normed_tok = normed(tokens)
    project = fold_rows(normed_tok, lax.all_gather(bottom_qkv, "seq", axis=0, tiled=True))
    project = project.astype(jnp.bfloat16)
    queries = project[:, :model_width]
    key_vals = padded(project[:, model_width:], (("seq", 0),), half_win)
    allowed = window_mask(first_tok, tok_count, half_win, total_tok)
    attended = attend(queries, key_vals[:, :model_width], key_vals[:, model_width:], allowed, H)
    out_sum = fold_rows(attended, lax.all_gather(bottom_out, "seq", axis=0, tiled=True))
    lower_tok = (tokens.astype(jnp.float32) + out_sum).astype(jnp.bfloat16)
    pooled = jnp.mean(
        lower_tok.astype(jnp.float32).reshape(tok_count // POOL, POOL, model_width), axis=1
    ).astype(jnp.bfloat16)
    all_units = lax.all_gather(pooled, "seq", axis=0, tiled=True)
    unit_norm = normed(all_units)
    top_q = jnp.dot(unit_norm, top_qkv[:, 0, :], preferred_element_type=jnp.float32).astype(
        jnp.bfloat16
    )
    top_k = jnp.dot(unit_norm, top_qkv[:, 1, :], preferred_element_type=jnp.float32).astype(
        jnp.bfloat16
    )
    top_v = jnp.dot(unit_norm, top_qkv[:, 2, :], preferred_element_type=jnp.float32).astype(
        jnp.bfloat16
    )
    top_att = attend(top_q, top_k, top_v, None, local_heads)
    head_term = jnp.dot(top_att, top_out, preferred_element_type=jnp.float32)
    head_total = lax.psum(head_term.astype(jnp.bfloat16), "seq").astype(jnp.float32)
    top_units = (all_units.astype(jnp.float32) + head_total).astype(jnp.bfloat16)
    upper_norm = normed(top_units)
    part_keys = jnp.dot(upper_norm, cross_kv[:, 0, :], preferred_element_type=jnp.float32).astype(
        jnp.bfloat16
    )
    part_vals = jnp.dot(upper_norm, cross_kv[:, 1, :], preferred_element_type=jnp.float32).astype(
        jnp.bfloat16
    )
    stacked = jnp.concatenate([part_keys, part_vals], axis=1)
    gathered = lax.all_gather(stacked, "seq", axis=1, tiled=True)
    unit_count = gathered.shape[0]
    arranged = gathered.reshape(unit_count, devices_seq, 2, part_keys.shape[1])
    cross_keys = arranged[:, :, 0, :].reshape(unit_count, model_width)
    cross_vals = arranged[:, :, 1, :].reshape(unit_count, model_width)
    lower_norm = normed(lower_tok)
    query_acc = fold_rows(lower_norm, lax.all_gather(cross_query, "seq", axis=0, tiled=True))
    cross_q = query_acc.astype(jnp.bfloat16)
    cross_att = attend(cross_q, cross_keys, cross_vals, None, H)
    cross_sum = fold_rows(cross_att, lax.all_gather(cross_out, "seq", axis=0, tiled=True))
    return (lower_tok.astype(jnp.float32) + cross_sum).astype(jnp.bfloat16)


def solution(mesh):
    in_specs = (
        P(("doc", "seq"), None),
        P("seq", None),
        P("seq", None),
        P(None, None, "seq"),
        P("seq", None),
        P("seq", None),
        P(None, None, "seq"),
        P("seq", None),
    )
    out_specs = P(("doc", "seq"), None)
    return jax.shard_map(local, mesh=mesh, in_specs=in_specs, out_specs=out_specs, check_vma=False)
```

profile of v0, /device:TPU:1, one launch (start us, length us, event | category | flops | bytes accessed | tf_op | source)
XLA Modules:
  0.0 322.5 jit_solution(8568578363218023782)
XLA Ops:
  6.5 0.7 all-gather.5.cloned.1.call-update
  7.3 0.7 all-gather.7.cloned.1.call-update
  8.1 1.2 fusion.39
  9.3 55.6 %all-gather.5.cloned.1.call-done = bf16[1024,3072]{1,0:T(8,128)(2,1)} async-done(((bf16[64,3072]{1,0:T(8,128)(2,1)}), bf16[1024,3072]{1,0:T(8,128)(2,1)}) %all-gather.5.cloned.1.call-update) | async-done | bytes 6291472 | tf_op jit(solution)/shard_map/all_gather | solution.py:87
  64.9 4.8 %convolution_convert_fusion = bf16[256,3072]{1,0:T(8,128)(2,1)S(1)} fusion(bf16[1024,3072]{1,0:T(8,128)(2,1)} %all-gather.5.cloned.1.call-done, bf16[256,1024]{1,0:T(8,128)(2,1)} %param.12, f32[256]{0:T(256)S(1)} %add_rsqrt_fusion.1), kind=kOutput, calls=%fused_computation.40 | convolution fusion | flops 1612185600 | bytes 8389632 | tf_op jit(solution)/shard_map/dot_general | solution.py:76
  69.8 2.7 collective-permute-start
  72.5 2.6 collective-permute-start.1
  75.3 1.0 copy.15
  76.3 10.8 %collective-permute-done = bf16[256,2048]{1,0:T(8,128)(2,1)} collective-permute-done((bf16[256,2048]{1,0:T(8,128)(2,1)S(1)}, bf16[256,2048]{1,0:T(8,128)(2,1)}, u32[]{:S(2)}, u32[]{:S(2)}) %collective-permute-start) | collective-permute-done | bytes 1048608 | tf_op jit(solution)/shard_map/ppermute | solution.py:24
  87.1 6.1 %collective-permute-done.1 = bf16[256,2048]{1,0:T(8,128)(2,1)} collective-permute-done((bf16[256,2048]{1,0:T(8,128)(2,1)S(1)}, bf16[256,2048]{1,0:T(8,128)(2,1)}, u32[]{:S(2)}, u32[]{:S(2)}) %collective-permute-start.1) | collective-permute-done | bytes 1048608 | tf_op jit(solution)/shard_map/ppermute | solution.py:26
  93.2 1.7 pad_maximum_fusion
  95.2 1.6 copy.16
  96.8 0.7 copy.17
  97.6 33.1 %while.26 = (s32[]{:T(128)}, bf16[16,256,64]{1,2,0:T(8,128)(2,1)S(1)}, bf16[16,256,64]{1,2,0:T(8,128)(2,1)}, bf16[16,768,64]{1,2,0:T(8,128)(2,1)}, bf16[16,768,6...) while((s32[]{:T(128)}, ...), condition=%wide.region_4.5_spmd.clone, body=%wide.region_1.4_spmd.clone.sunk | while | flops 52723200 | bytes 2633565 | solution.py:71
  97.6 1.4 fusion.111
  99.3 0.4 fusion.113
  99.7 1.4 fusion.111
  101.4 0.4 fusion.113
  101.8 1.4 fusion.111
  103.4 0.4 fusion.113
  103.8 1.4 fusion.111
  105.9 1.4 fusion.111
  108.0 1.4 fusion.111
  110.0 1.4 fusion.111
  112.1 1.4 fusion.111
  114.1 1.4 fusion.111
  116.2 1.4 fusion.111
  118.3 1.4 fusion.111
  120.3 1.4 fusion.111
  122.4 1.4 fusion.111
  124.5 1.4 fusion.111
  126.5 1.4 fusion.111
  128.6 1.4 fusion.111
  130.7 2.4 bitcast_reduce_fusion
  133.1 16.1 %all_gather.21 = bf16[128,1024]{1,0:T(8,128)(2,1)S(1)} all-gather(bf16[8,1024]{1,0:T(8,128)(2,1)S(1)} %multiply_convert_fusion.2), channel_id=1, replica_groups=mesh['doc'=32,'seq'=16] {'seq'}, dimensions={0}, use_global_device_ids=true | all-gather | bytes 278528 | tf_op jit(solution)/shard_map/all_gather | solution.py:98
  149.7 0.4 fusion.80
  150.1 0.4 fusion.38
  150.6 0.9 convolution_convert_fusion.2
  151.6 0.5 all-gather.11.cloned.1.call-update
  152.4 2.3 convolution_convert_fusion.1
  154.9 112.5 %all-reduce.2.cloned.1.call-done = bf16[128,1024]{1,0:T(8,128)(2,1)} async-done(((bf16[128,1024]{1,0:T(8,128)(2,1)}), bf16[128,1024]{1,0:T(8,128)(2,1)}) %all-reduce.2.cloned.1.call-update) | async-done | bytes 262160 | tf_op jit(solution)/shard_map/psum | solution.py:111
  267.4 1.1 fusion.41
  268.6 1.2 convolution_convert_fusion.7
  269.8 1.2 convolution_convert_fusion.6
  271.1 16.9 %all_gather.22 = bf16[128,2048]{0,1:T(8,128)(2,1)S(1)} all-gather(bf16[128,128]{0,1:T(8,128)(2,1)S(1)} %pad_maximum_fusion.1), channel_id=1, replica_groups=mesh['doc'=32,'seq'=16] {'seq'}, dimensions={1}, use_global_device_ids=true | all-gather | bytes 557056 | tf_op jit(solution)/shard_map/all_gather | solution.py:121
  288.7 7.1 %while.25 = (s32[]{:T(128)}, bf16[16,256,64]{1,2,0:T(8,128)(2,1)S(1)}, bf16[16,256,64]{1,2,0:T(8,128)(2,1)S(1)}, bf16[16,128,64]{2,1,0:T(8,128)(2,1)S(1)}, bf16[16,128,64]{2,1,0:T(8,128)(2,1)S(1)}, /*index=5*/s32[]{:T(128)}) while((s32[]{:T(128)}, bf16[16,256,64]{1,2,0:T(8,128)(2,1)S(1)}, bf16[16,256,64]{1,2,0:T(8,128)(2,1)S(1)}, ...), condition=%wide.region_15.16_spmd, body=%wide.region_12.15_spmd.sunk | while | flops 8617474 | bytes 531525 | solution.py:71
  295.8 17.0 %all-gather.11.cloned.1.call-done = bf16[1024,1024]{1,0:T(8,128)(2,1)} async-done(((bf16[64,1024]{1,0:T(8,128)(2,1)}), bf16[1024,1024]{1,0:T(8,128)(2,1)}) %all-gather.11.cloned.1.call-update) | async-done | bytes 2097168 | tf_op jit(solution)/shard_map/all_gather | solution.py:130
  312.8 3.1 fusion.37
  (116 shorter events, 18.5 us)
Async XLA Ops:
  6.5 144.0 %copy-start = (bf16[64,1024]{1,0:T(8,128)(2,1)S(1)}, bf16[64,1024]{1,0:T(8,128)(2,1)}, u32[]{:S(2)}) copy-start(bf16[64,1024]{1,0:T(8,128)(2,1)} %param.16) | copy-start | bytes 393220
  6.5 58.4 %all-gather.5.cloned.1.call-start = ((), (), s32[]{:S(2)}) async-start(), calls=%async_computation | async-start | bytes 6684672 | tf_op jit(solution)/shard_map/all_gather | solution.py:87
  7.3 123.4 %all-gather.7.cloned.1.call-start = ((), (), s32[]{:S(2)}) async-start(), calls=%async_computation.1 | async-start | bytes 2228224 | tf_op jit(solution)/shard_map/all_gather | solution.py:93
  8.0 144.4 %all-gather.9.cloned.1.call-start = ((), (), s32[]{:S(2)}) async-start(), calls=%async_computation.2 | async-start | bytes 2228224 | tf_op jit(solution)/shard_map/all_gather | solution.py:127
  69.8 17.2 %collective-permute-start = (bf16[256,2048]{1,0:T(8,128)(2,1)S(1)}, bf16[256,2048]{1,0:T(8,128)(2,1)}, u32[]{:S(2)}, u32[]{:S(2)}) collective-permute-start(bf16[256,2048]{1,0:T(8,128)(2,1)S(1)} %slice.45), channel_id=1, source_target_pairs={{0,1},{1,2},{2,3},{3,4},{4,5},{5,6},{6,7},{7,8},{8,9},{9,10},{10,1... | collective-permute-start | bytes 3145736 | tf_op jit(solution)/shard_map/ppermute | solution.py:24
  72.5 20.7 %collective-permute-start.1 = (bf16[256,2048]{1,0:T(8,128)(2,1)S(1)}, bf16[256,2048]{1,0:T(8,128)(2,1)}, u32[]{:S(2)}, u32[]{:S(2)}) collective-permute-start(bf16[256,2048]{1,0:T(8,128)(2,1)S(1)} %slice.45), channel_id=1, source_target_pairs={{1,0},{2,1},{3,2},{4,3},{5,4},{6,5},{7,6},{8,7},{9,8},{10,9},{11,1... | collective-permute-start | bytes 3145736 | tf_op jit(solution)/shard_map/ppermute | solution.py:26
  75.2 192.3 %all-reduce.2.cloned.1.call-start = ((), (), s32[]{:S(2)}) async-start(), calls=%async_computation.3 | async-start | bytes 524288 | tf_op jit(solution)/shard_map/psum | solution.py:111
  97.6 33.1 %copy-start.1 = (bf16[256,1024]{1,0:T(8,128)(2,1)S(1)}, bf16[256,1024]{1,0:T(8,128)(2,1)}, u32[]{:S(2)}) copy-start(bf16[256,1024]{1,0:T(8,128)(2,1)} %param.12) | copy-start | bytes 1572868
  130.7 18.7 %copy-start.2 = (bf16[1024,3,64]{0,2,1:T(8,128)(2,1)S(1)}, bf16[1024,3,64]{0,2,1:T(8,128)(2,1)}, u32[]{:S(2)}) copy-start(bf16[1024,3,64]{0,2,1:T(8,128)(2,1)} %param.15) | copy-start | bytes 1179652
  151.5 161.3 %all-gather.11.cloned.1.call-start = ((), (), s32[]{:S(2)}) async-start(), calls=%async_computation.4 | async-start | bytes 2228224 | tf_op jit(solution)/shard_map/all_gather | solution.py:130
  152.3 116.3 %copy-start.3 = (bf16[1024,2,64]{0,2,1:T(8,128)(2,1)S(1)}, bf16[1024,2,64]{0,2,1:T(8,128)(2,1)}, u32[]{:S(2)}) copy-start(bf16[1024,2,64]{0,2,1:T(8,128)(2,1)} %param.18) | copy-start | bytes 786436
Sparse Core Ops, SparseCore 0:
  9.5 55.3 all-gather.4
  67.0 41.1 all-gather.6
  110.3 42.0 all-gather.8
  154.6 112.8 all-reduce.1
  269.6 43.1 all-gather.10
where the time goes:
time: 323 us; the launch traced here: 322 us
  waiting for transfers between devices  204 us (63%)
  matrix products  51.4 us (16%)
  blocking collectives  33 us (10%)
  between operations  13.4 us (4%)
  other arithmetic  9.66 us (3%)
  starting transfers between devices  5.46 us (2%)
  local copies, waits for them, and re-layouts  4.62 us (1%)
    psum x1, waiting for transfers between devices, local(): lax.psum(head_term.astype(jnp.bfloat16), 'seq').astype(jnp.float32)  113 us
    all_gather x1, waiting for transfers between devices, local(): lax.all_gather(bottom_qkv, 'seq', axis=0, tiled=True)  55.6 us
    dot_general x33, matrix products, one_head(): jnp.dot(query_h, key_h.T, preferred_element_type=jnp.float32) * score_scale  25.3 us
    all_gather x1, waiting for transfers between devices, local(): lax.all_gather(cross_out, 'seq', axis=0, tiled=True)  17 us
    all_gather x1, blocking collectives, local(): gathered = lax.all_gather(stacked, 'seq', axis=1, tiled=True)  16.9 us
    all_gather x1, blocking collectives, local(): all_units = lax.all_gather(pooled, 'seq', axis=0, tiled=True)  16.1 us
    dot_general x4, matrix products, fold_rows(): return jnp.dot(operand, shard_rows, preferred_element_type=jnp.float32)  12.7 us
    ppermute x1, waiting for transfers between devices, padded(): lax.ppermute(tail, axis, [(i, (i + 1) % count) for i in range(ends)])  10.8 us
  transfers between devices with their start and end apart: 7, of which 6 were waited for; matrix products, arithmetic and copies ran while one was open for 19% of the time, Pallas kernels for 0%

commit v1 on v0

v1 whole, which is shorter than its diff:
```python
import math

import jax
import jax.numpy as jnp
from jax import lax
from jax.experimental import pallas as pl
from jax.experimental.pallas import tpu as pltpu
from jax.sharding import PartitionSpec as P

POOL = 32
EPS = 1e-06
F32 = jnp.float32
BF16 = jnp.bfloat16
EXP_SCALE = math.log2(math.e) / 8.0
MESH = pl.DeviceIdType.MESH
BO, CQ, TO, CO = 0, 1, 2, 3
NEAREST = (1, 7, 2, 6, 3, 5, 4)


def nt(a, b):
    return lax.dot_general(a, b, (((1,), (1,)), ((), ())), preferred_element_type=F32)


def nn(a, b):
    return jnp.dot(a, b, preferred_element_type=F32)


def norm(v):
    return (v * lax.rsqrt(jnp.mean(v * v, axis=-1, keepdims=True) + EPS)).astype(BF16)


def kernel(
    tok, w_qkv, w_bo, w_cq, w_to, w_co, tqt, ckt, out,
    wq, w2, xr, acc, qb, kv, bias, at, lt, pooled, tat, ckv, cq,
    ring_s, ring_r, par_s, par_r, own_s, halo_s, halo_r, cast_s, cast_r, fwd_s, fwd_r,
):
    me = lax.axis_index("seq")
    z, c = me // 2, me % 2
    partner = 2 * z + 1 - c

    def same(r):
        return 2 * ((z + r) % 8) + c

    left, right = (me + 15) % 16, (me + 1) % 16
    far = (me + 16 + (2 * c - 1)) % 16

    def slot_of(p):
        d = (p + 8 - z) % 8
        up = d // 4
        return (1 - up) * 2 * d + up * (15 - 2 * d)

    def remote(src, dst, s, r, to):
        return pltpu.make_async_remote_copy(
            src_ref=src, dst_ref=dst, send_sem=s, recv_sem=r,
            device_id={"seq": to}, device_id_type=MESH,
        )

    barrier = pltpu.get_barrier_semaphore()
    for peer in [same(r) for r in range(1, 8)] + [partner, far]:
        pl.semaphore_signal(barrier, inc=1, device_id={"seq": peer}, device_id_type=MESH)
    pl.semaphore_wait(barrier, 9)

    own = [w_qkv, w_bo, w_cq, w_to, w_co]

    def full(w):
        return wq if w == 0 else w2.at[w - 1]

    def ring_copy(w, h, d):
        buf = full(w)
        now = 2 * h - 1 if d == 0 else 2 * h
        if h == 4:
            now = 7
        if h == 1:
            src = own[w]
        else:
            src = buf.at[2 * (now - 2 if h < 4 else (5 if d == 0 else 6)) + c]
        dst = buf.at[2 * now + c]
        if h == 4:
            src, dst = src.at[pl.ds(32 * d, 32)], dst.at[pl.ds(32 * d, 32)]
        k = 2 * (h - 1) + d
        return remote(src, dst, ring_s.at[w, k], ring_r.at[w, k], same(1 if d == 0 else 7))

    def par_copy(w, s):
        buf = full(w)
        src = own[w] if s == 0 else buf.at[2 * s + c]
        return remote(src, buf.at[2 * s + c], par_s.at[w, s], par_r.at[w, s], partner)

    def own_copy(w):
        return pltpu.make_async_copy(own[w], full(w).at[c], own_s.at[w])

    def launch(w):
        ring_copy(w, 1, 0).start()
        ring_copy(w, 1, 1).start()
        par_copy(w, 0).start()
        own_copy(w).start()

    def hop(w, h):
        for d in (0, 1):
            ring_copy(w, h, d).wait_recv()
            if h < 4:
                ring_copy(w, h + 1, d).start()
                par_copy(w, 2 * h - 1 + d).start()
        if h == 4:
            par_copy(w, 7).start()

    def settle(w):
        own_copy(w).wait()
        for s in range(8):
            par_copy(w, s).wait_recv()

    launch(0)

    xn = norm(tok[...].astype(F32))
    for p in range(8):
        xr[slot_of(p)] = xn[:, 128 * p : 128 * p + 128]

    row = lax.broadcasted_iota(jnp.int32, (128, 640), 0)
    col = lax.broadcasted_iota(jnp.int32, (128, 640), 1)
    for b in range(2):
        pos = me * 256 - 256 + 128 * b + col
        ok = (col >= row) & (col < row + 512) & (pos >= 0) & (pos < 4096)
        bias[b] = jnp.where(ok, 0.0, -1e30).astype(F32)

    def qkv_group(g):
        lhs = jnp.concatenate([xr[2 * g], xr[2 * g + 1]], axis=1)

        def tile(n, _):
            cols = pl.ds(pl.multiple_of(n * 512, 512), 512)
            part = nn(lhs, wq[4 * g : 4 * g + 4, :, cols].reshape(256, 512))
            acc[n] = part if g == 0 else acc[n] + part
            return 0

        lax.fori_loop(0, 6, tile, 0)

    hop(0, 1)
    own_copy(0).wait()
    par_copy(0, 0).wait_recv()
    par_copy(0, 1).wait_recv()
    qkv_group(0)
    hop(0, 2)
    par_copy(0, 2).wait_recv()
    par_copy(0, 3).wait_recv()
    qkv_group(1)
    hop(0, 3)
    par_copy(0, 4).wait_recv()
    par_copy(0, 5).wait_recv()
    qkv_group(2)
    hop(0, 4)
    par_copy(0, 6).wait_recv()
    par_copy(0, 7).wait_recv()
    qkv_group(3)

    for n in range(4):
        block = acc[2 + n].astype(BF16)
        for j in range(4):
            kv[(4 * n + j) % 8, n // 2, 256:512, :] = block[:, 128 * j : 128 * j + 128]

    def halo(p, side):
        dst = kv.at[p, :, pl.ds(512 - 512 * side, 256), :]
        return remote(
            kv.at[p, :, pl.ds(256, 256), :], dst,
            halo_s.at[p, side], halo_r.at[p, side], left if side == 0 else right,
        )

    for n in range(2):
        block = acc[n].astype(BF16)
        for j in range(4):
            qb[4 * n + j] = block[:, 128 * j : 128 * j + 128]
    for p in range(8):
        halo(p, 0).start()
        halo(p, 1).start()
    launch(1 + BO)
    launch(1 + CQ)

    events = {
        1: lambda: hop(1 + BO, 1), 2: lambda: hop(1 + CQ, 1),
        3: lambda: hop(1 + BO, 2), 4: lambda: hop(1 + CQ, 2),
        5: lambda: hop(1 + BO, 3), 6: lambda: hop(1 + CQ, 3),
        7: lambda: hop(1 + BO, 4),
    }

    def attention(p, _):
        halo(p, 0).wait_recv()
        halo(p, 1).wait_recv()
        slot = slot_of(p)
        even = lax.broadcasted_iota(jnp.int32, (128, 128), 1) < 64
        for b in range(2):
            q = qb[p, 128 * b : 128 * b + 128, :]
            zero = jnp.zeros_like(q)
            both = jnp.concatenate([jnp.where(even, q, zero), jnp.where(even, zero, q)], axis=0)
            s = nt(both, kv[p, 0, 128 * b : 128 * b + 640, :])
            s = (s.reshape(2, 128, 640) + bias[b][None]).reshape(256, 640)
            e = jnp.exp2((s - jnp.max(s, axis=1, keepdims=True)) * EXP_SCALE)
            total = jnp.sum(e, axis=1, keepdims=True)
            o = nn(e.astype(BF16), kv[p, 1, 128 * b : 128 * b + 640, :]) / total
            at[slot, 128 * b : 128 * b + 128, :] = jnp.where(even, o[:128], o[128:]).astype(BF16)
        for k, event in events.items():
            pl.when(p == k)(event)
        return 0

    lax.fori_loop(0, 8, attention, 0)
    launch(1 + TO)
    launch(1 + CO)

    def square(lhs8, w, put):
        lhs = jnp.concatenate([lhs8[s] for s in range(8)], axis=1)

        def tile(n, _):
            cols = pl.ds(pl.multiple_of(n * 256, 256), 256)
            put(n, cols, nn(lhs, w2[w, :, :, cols].reshape(1024, 256)))
            return 0

        lax.fori_loop(0, 4, tile, 0)

    settle(1 + BO)

    def put_lower(n, cols, o):
        lt[:, cols] = (tok[:, cols].astype(F32) + o).astype(BF16)

    square(at, BO, put_lower)

    def cast_copies(b, buf):
        mine = buf.at[me]
        sends = [remote(mine, mine, cast_s.at[b, 0], cast_r.at[b, 0], partner)]
        for r in range(1, 8):
            sends.append(remote(mine, mine, cast_s.at[b, r], cast_r.at[b, r], same(r)))
        return sends

    def fwd_copy(b, buf, r):
        there = buf.at[same(8 - r)]
        return remote(there, there, fwd_s.at[b, r], fwd_r.at[b, r], partner)

    def cast_start(b, buf):
        sends = cast_copies(b, buf)
        for r in (4, 3, 5, 2, 6, 1, 7, 0):
            sends[r].start()

    def cast_finish(b, buf):
        sends = cast_copies(b, buf)
        for r in NEAREST:
            sends[r].wait_recv()
            fwd_copy(b, buf, r).start()
        sends[0].wait_recv()
        for r in NEAREST:
            fwd_copy(b, buf, r).wait_recv()

    low = lt[...].astype(F32)
    pooled[me] = (jnp.sum(low.reshape(8, POOL, 1024), axis=1) * (1.0 / POOL)).astype(BF16).astype(F32)
    cast_start(0, pooled)
    hop(1 + CQ, 4)
    ln = norm(low)
    for p in range(8):
        xr[slot_of(p)] = ln[:, 128 * p : 128 * p + 128]
    hop(1 + TO, 1)
    cast_finish(0, pooled)

    un = norm(pooled[...].reshape(128, 1024))
    tq = nt(un, tqt[0]).astype(BF16)
    tk = nt(un, tqt[1]).astype(BF16)
    tvt = nt(tqt[2], un).astype(BF16)
    st = nt(tk, tq)
    e = jnp.exp2((st - jnp.max(st, axis=0, keepdims=True)) * EXP_SCALE)
    tat[me] = (nn(tvt, e.astype(BF16)) / jnp.sum(e, axis=0, keepdims=True)).astype(BF16)
    cast_start(1, tat)
    hop(1 + CO, 1)
    hop(1 + TO, 2)
    settle(1 + CQ)

    def put_query(n, cols, o):
        o = o.astype(BF16)
        cq[2 * n] = o[:, :128]
        cq[2 * n + 1] = o[:, 128:]

    square(xr, CQ, put_query)
    hop(1 + CO, 2)
    hop(1 + TO, 3)
    cast_finish(1, tat)
    hop(1 + CO, 3)
    hop(1 + TO, 4)
    settle(1 + TO)

    units = pooled[...].reshape(128, 1024)
    chips = []
    for s in range(8):
        off = (s + 1) // 2 * (1 - 2 * (s % 2))
        base = 2 * ((z + 8 + off) % 8)
        chips.append(tat[pl.ds(base, 2)].reshape(128, 128).T)
    ta = jnp.concatenate(chips, axis=1)
    units = units + nn(ta, w2[TO].reshape(1024, 1024))
    up = norm(units.astype(BF16).astype(F32))
    ckv[me, 0] = nt(ckt[0], up).astype(BF16)
    ckv[me, 1] = nt(ckt[1], up).astype(BF16)
    cast_start(2, ckv)
    hop(1 + CO, 4)
    settle(1 + CO)
    cast_finish(2, ckv)

    def cross(p, _):
        q = cq[p]
        even = lax.broadcasted_iota(jnp.int32, (256, 128), 1) < 64
        zero = jnp.zeros_like(q)
        both = jnp.concatenate([jnp.where(even, q, zero), jnp.where(even, zero, q)], axis=0)
        s = nn(both, ckv[pl.ds(2 * p, 2), 0].reshape(128, 128))
        e = jnp.exp2((s - jnp.max(s, axis=1, keepdims=True)) * EXP_SCALE)
        total = jnp.sum(e, axis=1, keepdims=True)
        o = nt(e.astype(BF16), ckv[pl.ds(2 * p, 2), 1].reshape(128, 128)) / total
        at[slot_of(p)] = jnp.where(even, o[:256], o[256:]).astype(BF16)
        return 0

    lax.fori_loop(0, 8, cross, 0)

    def put_out(n, cols, o):
        out[:, cols] = (lt[:, cols].astype(F32) + o).astype(BF16)

    square(at, CO, put_out)

    for w in range(5):
        for h in range(1, 5):
            ring_copy(w, h, 0).wait_send()
            ring_copy(w, h, 1).wait_send()
        for s in range(8):
            par_copy(w, s).wait_send()
    for p in range(8):
        halo(p, 0).wait_send()
        halo(p, 1).wait_send()
    for b, buf in enumerate((pooled, tat, ckv)):
        for copy in cast_copies(b, buf):
            copy.wait_send()
        for r in range(1, 8):
            fwd_copy(b, buf, r).wait_send()


def local(tokens, bottom_qkv, bottom_out, top_qkv, top_out, cross_query, cross_kv, cross_out):
    tqt = top_qkv.transpose(1, 2, 0)
    ckt = cross_kv.transpose(1, 2, 0)
    dma = pltpu.SemaphoreType.DMA
    return pl.pallas_call(
        kernel,
        out_shape=jax.ShapeDtypeStruct((256, 1024), BF16),
        in_specs=[pl.BlockSpec(memory_space=pltpu.VMEM)] * 8,
        out_specs=pl.BlockSpec(memory_space=pltpu.VMEM),
        scratch_shapes=[
            pltpu.VMEM((16, 64, 3072), BF16),
            pltpu.VMEM((4, 16, 64, 1024), BF16),
            pltpu.VMEM((8, 256, 128), BF16),
            pltpu.VMEM((6, 256, 512), F32),
            pltpu.VMEM((8, 256, 128), BF16),
            pltpu.VMEM((8, 2, 768, 128), BF16),
            pltpu.VMEM((2, 128, 640), F32),
            pltpu.VMEM((8, 256, 128), BF16),
            pltpu.VMEM((256, 1024), BF16),
            pltpu.VMEM((16, 8, 1024), F32),
            pltpu.VMEM((16, 64, 128), BF16),
            pltpu.VMEM((16, 2, 64, 128), BF16),
            pltpu.VMEM((8, 256, 128), BF16),
            dma((5, 8)), dma((5, 8)), dma((5, 8)), dma((5, 8)), dma((5,)),
            dma((8, 2)), dma((8, 2)),
            dma((3, 8)), dma((3, 8)), dma((3, 8)), dma((3, 8)),
        ],
        compiler_params=pltpu.CompilerParams(
            collective_id=0, has_side_effects=True, vmem_limit_bytes=60 * 1024 * 1024
        ),
        name="layer",
    )(tokens, bottom_qkv, bottom_out, cross_query, top_out, cross_out, tqt, ckt)


def solution(mesh):
    in_specs = (
        P(("doc", "seq"), None),
        P("seq", None),
        P("seq", None),
        P(None, None, "seq"),
        P("seq", None),
        P("seq", None),
        P(None, None, "seq"),
        P("seq", None),
    )
    out_specs = P(("doc", "seq"), None)
    return jax.shard_map(local, mesh=mesh, in_specs=in_specs, out_specs=out_specs, check_vma=False)
```

time: 323 us -> 135 us (0.42)
  waiting for transfers between devices: 204 us -> 0 us
  Pallas kernels: 0 us -> 133 us
  matrix products: 51.4 us -> 0 us
  blocking collectives: 33 us -> 0 us
  between operations: 13.4 us -> 0.01 us
  other arithmetic: 9.66 us -> 0 us
  starting transfers between devices: 5.46 us -> 0 us
    pallas_call x0 -> x1, Pallas kernels: none -> 133 us  [local(): pl.pallas_call(kernel, out_shape=jax.ShapeDtypeStruct((256, 1024), BF16),...]
    psum x1 -> x0, waiting for transfers between devices: 113 us -> none  [local(): lax.psum(head_term.astype(jnp.bfloat16), 'seq').astype(jnp.float32)]
    all_gather x4 -> x0, waiting for transfers between devices: 72.7 us -> none  [the longest x1 55.6 us: local(): lax.all_gather(bottom_qkv, 'seq', axis=0, tiled=True)]
    dot_general x74 -> x0, matrix products: 51.4 us -> none  [the longest x33 25.3 us: one_head(): jnp.dot(query_h, key_h.T, preferred_element_type=jnp.float32) * score_scale]
    all_gather x2 -> x0, blocking collectives: 33 us -> none  [the longest x1 16.9 us: local(): gathered = lax.all_gather(stacked, 'seq', axis=1, tiled=True)]
    ppermute x2 -> x0, waiting for transfers between devices: 16.9 us -> none  [the longest x1 10.8 us: padded(): lax.ppermute(tail, axis, [(i, (i + 1) % count) for i in range(ends)])]
    reduce_sum x37 -> x0, other arithmetic: 7.91 us -> none  [the longest x33 5.29 us: one_head(): row_total = jnp.sum(expo, axis=1, keepdims=True)]
    ppermute x2 -> x0, starting transfers between devices: 5.29 us -> none  [the longest x1 2.69 us: padded(): lax.ppermute(tail, axis, [(i, (i + 1) % count) for i in range(ends)])]
  transfers between devices with their start and end apart: 7 -> 0, of which waited for: 6 -> 0; matrix products, arithmetic and copies ran while one was open for 19% -> 0% of each run, Pallas kernels for 0% -> 0%
where the time goes in v1:
time: 135 us
  Pallas kernels  133 us (99%)
  local copies, waits for them, and re-layouts  1.87 us (1%)
    pallas_call x1, Pallas kernels, local(): pl.pallas_call(kernel, out_shape=jax.ShapeDtypeStruct((256, 1024), BF16),...  133 us

profile of v1, /device:TPU:1, one launch (start us, length us, event | category | flops | bytes accessed | tf_op | source)
XLA Modules:
  0.0 134.8 jit_solution(1262342005139535298)
XLA Ops:
  0.0 132.9 %layer.1 = bf16[256,1024]{1,0:T(8,128)(2,1)} custom-call(bf16[256,1024]{1,0:T(8,128)(2,1)} %tok.1, bf16[64,3072]{1,0:T(8,128)(2,1)} %w_qkv.1, bf16[64,1024]{1,0:T(8,128)(2,1)} %w_bo.1, bf16[64,1024]{1,0:T(8,128)(2,1)} %w_cq.1, bf16[64,1024]{1,0:T(8,128)(2,1)} %w_to.1, bf16[64,1024]{1,0:T(8,128)(2,1)} %w_co.1, bf16[3,64,1024]{2,1,0:T(8,128)(2,1)} %bitcast.2, ...), custom_call_target="tpu_custom_call" | custom-call | tf_op jit(solution)/shard_map/layer/pallas_call | solution.py:337
  132.9 1.9 %copy.10 = bf16[256,1024]{1,0:T(8,128)(2,1)} copy(bf16[256,1024]{1,0:T(8,128)(2,1)} %layer.1) | data formatting | bytes 1048576

commit v2 on v1

--- a/solution.py
+++ b/solution.py
@@ -31,8 +31,9 @@
 
 def kernel(
     tok, w_qkv, w_bo, w_cq, w_to, w_co, tqt, ckt, out,
-    wq, w2, xr, acc, qb, kv, bias, at, lt, pooled, tat, ckv, cq,
+    wq, w2, xr, acc, qb, kv, bias, at, lt, pooled, tat, ckv, cq, tokh, xh, acch,
     ring_s, ring_r, par_s, par_r, own_s, halo_s, halo_r, cast_s, cast_r, fwd_s, fwd_r,
+    side_s, side_r, tok_s, tok_r,
 ):
     me = lax.axis_index("seq")
     z, c = me // 2, me % 2
@@ -41,7 +42,10 @@
     def same(r):
         return 2 * ((z + r) % 8) + c
 
-    left, right = (me + 15) % 16, (me + 1) % 16
+    doc = lax.axis_index("doc")
+    x, y = doc % 4, doc // 4
+    half = (x + y) % 2
+    across = (4 * y + x + 1 - 2 * (x % 2), 4 * (y + 1 - 2 * (y % 2)) + x)
     far = (me + 16 + (2 * c - 1)) % 16
 
     def slot_of(p):
@@ -58,57 +62,88 @@
     barrier = pltpu.get_barrier_semaphore()
     for peer in [same(r) for r in range(1, 8)] + [partner, far]:
         pl.semaphore_signal(barrier, inc=1, device_id={"seq": peer}, device_id_type=MESH)
-    pl.semaphore_wait(barrier, 9)
+    for peer in across:
+        pl.semaphore_signal(barrier, inc=1, device_id={"doc": peer}, device_id_type=MESH)
+    pl.semaphore_wait(barrier, 11)
 
     own = [w_qkv, w_bo, w_cq, w_to, w_co]
 
     def full(w):
         return wq if w == 0 else w2.at[w - 1]
 
-    def ring_copy(w, h, d):
+    def arriving(h, d):
+        return 7 if h == 4 else 2 * h - 1 + d
+
+    def rows(buf, start):
+        return buf.at[pl.ds(pl.multiple_of(start, 16), 16)]
+
+    def ring_copy(w, h, d, i):
         buf = full(w)
-        now = 2 * h - 1 if d == 0 else 2 * h
-        if h == 4:
-            now = 7
-        if h == 1:
-            src = own[w]
+        src = own[w] if h == 1 else buf.at[2 * arriving(h - 1, d) + c]
+        dst = buf.at[2 * arriving(h, d) + c]
+        at_row = 32 * half + 16 * i
+        k = 4 * (h - 1) + 2 * d + i
+        return remote(
+            rows(src, at_row), rows(dst, at_row), ring_s.at[w, k], ring_r.at[w, k],
+            same(1 if d == 0 else 7),
+        )
+
+    def side_copy(w, s, i):
+        there = rows(full(w).at[2 * s + c], 32 * half + 16 * i)
+        return pltpu.make_async_remote_copy(
+            src_ref=there, dst_ref=there, send_sem=side_s.at[w, 2 * s + i],
+            recv_sem=side_r.at[w, 2 * s + i],
+            device_id={"doc": across[i]}, device_id_type=MESH,
+        )
+
+    def par_copy(w, s, j):
+        if s == 0:
+            src, dst = own[w], full(w).at[c]
         else:
-            src = buf.at[2 * (now - 2 if h < 4 else (5 if d == 0 else 6)) + c]
-        dst = buf.at[2 * now + c]
-        if h == 4:
-            src, dst = src.at[pl.ds(32 * d, 32)], dst.at[pl.ds(32 * d, 32)]
-        k = 2 * (h - 1) + d
-        return remote(src, dst, ring_s.at[w, k], ring_r.at[w, k], same(1 if d == 0 else 7))
-
-    def par_copy(w, s):
-        buf = full(w)
-        src = own[w] if s == 0 else buf.at[2 * s + c]
-        return remote(src, buf.at[2 * s + c], par_s.at[w, s], par_r.at[w, s], partner)
+            at_row = 32 * half + 16 * j if j < 2 else 32 * (1 - half) + 16 * (j - 2)
+            src = dst = rows(full(w).at[2 * s + c], at_row)
+        return remote(src, dst, par_s.at[w, 4 * s + j], par_r.at[w, 4 * s + j], partner)
 
     def own_copy(w):
         return pltpu.make_async_copy(own[w], full(w).at[c], own_s.at[w])
 
+    def chunks(h):
+        return [(d, i) for i in (0, 1) for d in (0, 1) if h < 4 or i == d]
+
     def launch(w):
-        ring_copy(w, 1, 0).start()
-        ring_copy(w, 1, 1).start()
-        par_copy(w, 0).start()
+        for d, i in chunks(1):
+            ring_copy(w, 1, d, i).start()
+        par_copy(w, 0, 0).start()
         own_copy(w).start()
 
     def hop(w, h):
-        for d in (0, 1):
-            ring_copy(w, h, d).wait_recv()
-            if h < 4:
-                ring_copy(w, h + 1, d).start()
-                par_copy(w, 2 * h - 1 + d).start()
-        if h == 4:
-            par_copy(w, 7).start()
+        for d, i in chunks(h):
+            ring_copy(w, h, d, i).wait_recv()
+            if h < 4 and (d, i) in chunks(h + 1):
+                ring_copy(w, h + 1, d, i).start()
+            side_copy(w, arriving(h, d), i).start()
+            par_copy(w, arriving(h, d), i).start()
+
+    def lag(w, h):
+        for d, i in chunks(h):
+            side_copy(w, arriving(h, d), i).wait_recv()
+            par_copy(w, arriving(h, d), 2 + i).start()
+
+    def have(w, s):
+        if s == 0:
+            own_copy(w).wait()
+            par_copy(w, 0, 0).wait_recv()
+        else:
+            for j in range(4):
+                par_copy(w, s, j).wait_recv()
 
     def settle(w):
-        own_copy(w).wait()
         for s in range(8):
-            par_copy(w, s).wait_recv()
+            have(w, s)
 
     launch(0)
+    tok_copy = remote(tok, tokh, tok_s, tok_r, far)
+    tok_copy.start()
 
     xn = norm(tok[...].astype(F32))
     for p in range(8):
@@ -122,44 +157,64 @@
         bias[b] = jnp.where(ok, 0.0, -1e30).astype(F32)
 
     def qkv_group(g):
-        lhs = jnp.concatenate([xr[2 * g], xr[2 * g + 1]], axis=1)
-
-        def tile(n, _):
+        mine = jnp.concatenate([xr[2 * g], xr[2 * g + 1]], axis=1)
+        both = jnp.concatenate(
+            [mine, jnp.concatenate([xh[2 * g], xh[2 * g + 1]], axis=1)], axis=0
+        )
+
+        def tile_q(n, _):
             cols = pl.ds(pl.multiple_of(n * 512, 512), 512)
-            part = nn(lhs, wq[4 * g : 4 * g + 4, :, cols].reshape(256, 512))
+            part = nn(mine, wq[4 * g : 4 * g + 4, :, cols].reshape(256, 512))
             acc[n] = part if g == 0 else acc[n] + part
             return 0
 
-        lax.fori_loop(0, 6, tile, 0)
+        def tile_kv(n, _):
+            cols = pl.ds(pl.multiple_of(1024 + n * 512, 512), 512)
+            part = nn(both, wq[4 * g : 4 * g + 4, :, cols].reshape(256, 512))
+            acch[n] = part if g == 0 else acch[n] + part
+            return 0
+
+        lax.fori_loop(0, 4, tile_kv, 0)
+        lax.fori_loop(0, 2, tile_q, 0)
 
     hop(0, 1)
-    own_copy(0).wait()
-    par_copy(0, 0).wait_recv()
-    par_copy(0, 1).wait_recv()
+    hop(0, 2)
+    lag(0, 1)
+    tok_copy.wait_recv()
+    xn = norm(tokh[...].astype(F32))
+    for p in range(8):
+        xh[slot_of(p)] = xn[:, 128 * p : 128 * p + 128]
+    have(0, 0)
+    have(0, 1)
     qkv_group(0)
-    hop(0, 2)
-    par_copy(0, 2).wait_recv()
-    par_copy(0, 3).wait_recv()
+    hop(0, 3)
+    lag(0, 2)
+    have(0, 2)
+    have(0, 3)
     qkv_group(1)
-    hop(0, 3)
-    par_copy(0, 4).wait_recv()
-    par_copy(0, 5).wait_recv()
+    hop(0, 4)
+    launch(1 + BO)
+    launch(1 + CQ)
+    lag(0, 3)
+    have(0, 4)
+    have(0, 5)
     qkv_group(2)
-    hop(0, 4)
-    par_copy(0, 6).wait_recv()
-    par_copy(0, 7).wait_recv()
+    lag(0, 4)
+    have(0, 6)
+    have(0, 7)
     qkv_group(3)
 
+    far_rows = pl.ds(pl.multiple_of(512 * c, 256), 256)
     for n in range(4):
-        block = acc[2 + n].astype(BF16)
+        block = acch[n].astype(BF16)
         for j in range(4):
-            kv[(4 * n + j) % 8, n // 2, 256:512, :] = block[:, 128 * j : 128 * j + 128]
-
-    def halo(p, side):
-        dst = kv.at[p, :, pl.ds(512 - 512 * side, 256), :]
+            kv[(4 * n + j) % 8, n // 2, 256:512, :] = block[:256, 128 * j : 128 * j + 128]
+            kv[(4 * n + j) % 8, n // 2, far_rows, :] = block[256:, 128 * j : 128 * j + 128]
+
+    def halo(p):
         return remote(
-            kv.at[p, :, pl.ds(256, 256), :], dst,
-            halo_s.at[p, side], halo_r.at[p, side], left if side == 0 else right,
+            kv.at[p, :, pl.ds(256, 256), :], kv.at[p, :, far_rows, :],
+            halo_s.at[p], halo_r.at[p], partner,
         )
 
     for n in range(2):
@@ -167,21 +222,24 @@
         for j in range(4):
             qb[4 * n + j] = block[:, 128 * j : 128 * j + 128]
     for p in range(8):
-        halo(p, 0).start()
-        halo(p, 1).start()
-    launch(1 + BO)
-    launch(1 + CQ)
+        halo(p).start()
+
+    def event(*steps):
+        def run():
+            for step, w, *h in steps:
+                step(1 + w, *h)
+        return run
 
     events = {
-        1: lambda: hop(1 + BO, 1), 2: lambda: hop(1 + CQ, 1),
-        3: lambda: hop(1 + BO, 2), 4: lambda: hop(1 + CQ, 2),
-        5: lambda: hop(1 + BO, 3), 6: lambda: hop(1 + CQ, 3),
-        7: lambda: hop(1 + BO, 4),
+        0: event((hop, BO, 1)), 1: event((hop, CQ, 1)),
+        2: event((hop, BO, 2), (lag, BO, 1)), 3: event((hop, CQ, 2), (lag, CQ, 1)),
+        4: event((hop, BO, 3), (lag, BO, 2)), 5: event((hop, CQ, 3), (lag, CQ, 2)),
+        6: event((hop, BO, 4), (lag, BO, 3), (hop, CQ, 4), (lag, CQ, 3), (launch, TO), (launch, CO)),
+        7: event((lag, BO, 4), (lag, CQ, 4)),
     }
 
     def attention(p, _):
-        halo(p, 0).wait_recv()
-        halo(p, 1).wait_recv()
+        halo(p).wait_recv()
         slot = slot_of(p)
         even = lax.broadcasted_iota(jnp.int32, (128, 128), 1) < 64
         for b in range(2):
@@ -199,8 +257,6 @@
         return 0
 
     lax.fori_loop(0, 8, attention, 0)
-    launch(1 + TO)
-    launch(1 + CO)
 
     def square(lhs8, w, put):
         lhs = jnp.concatenate([lhs8[s] for s in range(8)], axis=1)
@@ -247,7 +303,6 @@
     low = lt[...].astype(F32)
     pooled[me] = (jnp.sum(low.reshape(8, POOL, 1024), axis=1) * (1.0 / POOL)).astype(BF16).astype(F32)
     cast_start(0, pooled)
-    hop(1 + CQ, 4)
     ln = norm(low)
     for p in range(8):
         xr[slot_of(p)] = ln[:, 128 * p : 128 * p + 128]
@@ -264,6 +319,7 @@
     cast_start(1, tat)
     hop(1 + CO, 1)
     hop(1 + TO, 2)
+    lag(1 + TO, 1)
     settle(1 + CQ)
 
     def put_query(n, cols, o):
@@ -272,11 +328,16 @@
         cq[2 * n + 1] = o[:, 128:]
 
     square(xr, CQ, put_query)
+    hop(1 + TO, 3)
+    lag(1 + TO, 2)
     hop(1 + CO, 2)
-    hop(1 + TO, 3)
+    lag(1 + CO, 1)
+    hop(1 + TO, 4)
+    lag(1 + TO, 3)
     cast_finish(1, tat)
     hop(1 + CO, 3)
-    hop(1 + TO, 4)
+    lag(1 + CO, 2)
+    lag(1 + TO, 4)
     settle(1 + TO)
 
     units = pooled[...].reshape(128, 1024)
@@ -292,7 +353,8 @@
     ckv[me, 1] = nt(ckt[1], up).astype(BF16)
     cast_start(2, ckv)
     hop(1 + CO, 4)
-    settle(1 + CO)
+    lag(1 + CO, 3)
+    lag(1 + CO, 4)
     cast_finish(2, ckv)
 
     def cross(p, _):
@@ -309,20 +371,24 @@
 
     lax.fori_loop(0, 8, cross, 0)
 
+    settle(1 + CO)
+
     def put_out(n, cols, o):
         out[:, cols] = (lt[:, cols].astype(F32) + o).astype(BF16)
 
     square(at, CO, put_out)
 
     for w in range(5):
+        par_copy(w, 0, 0).wait_send()
         for h in range(1, 5):
-            ring_copy(w, h, 0).wait_send()
-            ring_copy(w, h, 1).wait_send()
-        for s in range(8):
-            par_copy(w, s).wait_send()
+            for d, i in chunks(h):
+                ring_copy(w, h, d, i).wait_send()
+                side_copy(w, arriving(h, d), i).wait_send()
+                par_copy(w, arriving(h, d), i).wait_send()
+                par_copy(w, arriving(h, d), 2 + i).wait_send()
+    tok_copy.wait_send()
     for p in range(8):
-        halo(p, 0).wait_send()
-        halo(p, 1).wait_send()
+        halo(p).wait_send()
     for b, buf in enumerate((pooled, tat, ckv)):
         for copy in cast_copies(b, buf):
             copy.wait_send()
@@ -343,7 +409,7 @@
             pltpu.VMEM((16, 64, 3072), BF16),
             pltpu.VMEM((4, 16, 64, 1024), BF16),
             pltpu.VMEM((8, 256, 128), BF16),
-            pltpu.VMEM((6, 256, 512), F32),
+            pltpu.VMEM((2, 256, 512), F32),
             pltpu.VMEM((8, 256, 128), BF16),
             pltpu.VMEM((8, 2, 768, 128), BF16),
             pltpu.VMEM((2, 128, 640), F32),
@@ -353,9 +419,13 @@
             pltpu.VMEM((16, 64, 128), BF16),
             pltpu.VMEM((16, 2, 64, 128), BF16),
             pltpu.VMEM((8, 256, 128), BF16),
-            dma((5, 8)), dma((5, 8)), dma((5, 8)), dma((5, 8)), dma((5,)),
-            dma((8, 2)), dma((8, 2)),
+            pltpu.VMEM((256, 1024), BF16),
+            pltpu.VMEM((8, 256, 128), BF16),
+            pltpu.VMEM((4, 512, 512), F32),
+            dma((5, 16)), dma((5, 16)), dma((5, 32)), dma((5, 32)), dma((5,)),
+            dma((8,)), dma((8,)),
             dma((3, 8)), dma((3, 8)), dma((3, 8)), dma((3, 8)),
+            dma((5, 16)), dma((5, 16)), dma, dma,
         ],
         compiler_params=pltpu.CompilerParams(
             collective_id=0, has_side_effects=True, vmem_limit_bytes=60 * 1024 * 1024

time: 135 us -> 115 us (0.85)
  Pallas kernels: 133 us -> 113 us
    pallas_call x1, Pallas kernels: 133 us -> 113 us  [local(): pl.pallas_call(kernel, out_shape=jax.ShapeDtypeStruct((256, 1024), BF16),...]
where the time goes in v2:
time: 115 us
  Pallas kernels  113 us (98%)
  local copies, waits for them, and re-layouts  1.87 us (2%)
    pallas_call x1, Pallas kernels, local(): pl.pallas_call(kernel, out_shape=jax.ShapeDtypeStruct((256, 1024), BF16),...  113 us

profile of v2, /device:TPU:1, one launch (start us, length us, event | category | flops | bytes accessed | tf_op | source)
XLA Modules:
  0.0 115.2 jit_solution(5333393289302463178)
XLA Ops:
  0.0 113.3 %layer.1 = bf16[256,1024]{1,0:T(8,128)(2,1)} custom-call(bf16[256,1024]{1,0:T(8,128)(2,1)} %tok.1, bf16[64,3072]{1,0:T(8,128)(2,1)} %w_qkv.1, bf16[64,1024]{1,0:T(8,128)(2,1)} %w_bo.1, bf16[64,1024]{1,0:T(8,128)(2,1)} %w_cq.1, bf16[64,1024]{1,0:T(8,128)(2,1)} %w_to.1, bf16[64,1024]{1,0:T(8,128)(2,1)} %w_co.1, bf16[3,64,1024]{2,1,0:T(8,128)(2,1)} %bitcast.2, ...), custom_call_target="tpu_custom_call" | custom-call | tf_op jit(solution)/shard_map/layer/pallas_call | solution.py:403
  113.3 1.9 %copy.10 = bf16[256,1024]{1,0:T(8,128)(2,1)} copy(bf16[256,1024]{1,0:T(8,128)(2,1)} %layer.1) | data formatting | bytes 1048576

commit v3 on v2

--- a/solution.py
+++ b/solution.py
@@ -30,10 +30,10 @@
 
 
 def kernel(
-    tok, w_qkv, w_bo, w_cq, w_to, w_co, tqt, ckt, out,
+    tok, w_qkv, w_bo, w_cq, w_to, w_co, tq_hbm, ck_hbm, out,
     wq, w2, xr, acc, qb, kv, bias, at, lt, pooled, tat, ckv, cq, tokh, xh, acch,
     ring_s, ring_r, par_s, par_r, own_s, halo_s, halo_r, cast_s, cast_r, fwd_s, fwd_r,
-    side_s, side_r, tok_s, tok_r,
+    side_s, side_r, tok_s, tok_r, tqt, ckt, unit_s,
 ):
     me = lax.axis_index("seq")
     z, c = me // 2, me % 2
@@ -59,6 +59,12 @@
             device_id={"seq": to}, device_id_type=MESH,
         )
 
+    unit_copies = (
+        pltpu.make_async_copy(tq_hbm, tqt, unit_s.at[0]),
+        pltpu.make_async_copy(ck_hbm, ckt, unit_s.at[1]),
+    )
+    for copy in unit_copies:
+        copy.start()
     barrier = pltpu.get_barrier_semaphore()
     for peer in [same(r) for r in range(1, 8)] + [partner, far]:
         pl.semaphore_signal(barrier, inc=1, device_id={"seq": peer}, device_id_type=MESH)
@@ -195,14 +201,18 @@
     hop(0, 4)
     launch(1 + BO)
     launch(1 + CQ)
+    launch(1 + TO)
     lag(0, 3)
     have(0, 4)
     have(0, 5)
     qkv_group(2)
     lag(0, 4)
+    hop(1 + BO, 1)
     have(0, 6)
     have(0, 7)
     qkv_group(3)
+    hop(1 + CQ, 1)
+    hop(1 + TO, 1)
 
     far_rows = pl.ds(pl.multiple_of(512 * c, 256), 256)
     for n in range(4):
@@ -230,12 +240,18 @@
                 step(1 + w, *h)
         return run
 
+    hop(1 + BO, 2)
+    lag(1 + BO, 1)
+    launch(1 + CO)
     events = {
-        0: event((hop, BO, 1)), 1: event((hop, CQ, 1)),
-        2: event((hop, BO, 2), (lag, BO, 1)), 3: event((hop, CQ, 2), (lag, CQ, 1)),
-        4: event((hop, BO, 3), (lag, BO, 2)), 5: event((hop, CQ, 3), (lag, CQ, 2)),
-        6: event((hop, BO, 4), (lag, BO, 3), (hop, CQ, 4), (lag, CQ, 3), (launch, TO), (launch, CO)),
-        7: event((lag, BO, 4), (lag, CQ, 4)),
+        0: event((hop, CQ, 2), (lag, CQ, 1)),
+        1: event((hop, TO, 2), (lag, TO, 1)),
+        2: event((hop, BO, 3), (lag, BO, 2)),
+        3: event((hop, CQ, 3), (lag, CQ, 2)),
+        4: event((hop, TO, 3), (lag, TO, 2)),
+        5: event((hop, CO, 1)),
+        6: event((hop, BO, 4), (lag, BO, 3)),
+        7: event((hop, CQ, 4), (lag, CQ, 3), (lag, BO, 4)),
     }
 
     def attention(p, _):
@@ -301,15 +317,25 @@
             fwd_copy(b, buf, r).wait_recv()
 
     low = lt[...].astype(F32)
-    pooled[me] = (jnp.sum(low.reshape(8, POOL, 1024), axis=1) * (1.0 / POOL)).astype(BF16).astype(F32)
+    pooled[me] = (jnp.sum(low.reshape(8, POOL, 1024), axis=1) * (1.0 / POOL)).astype(BF16)
     cast_start(0, pooled)
+    hop(1 + TO, 4)
+    lag(1 + TO, 3)
+    hop(1 + CO, 2)
+    lag(1 + CO, 1)
+    lag(1 + CQ, 4)
     ln = norm(low)
     for p in range(8):
         xr[slot_of(p)] = ln[:, 128 * p : 128 * p + 128]
-    hop(1 + TO, 1)
+    lag(1 + TO, 4)
+    hop(1 + CO, 3)
+    lag(1 + CO, 2)
     cast_finish(0, pooled)
 
-    un = norm(pooled[...].reshape(128, 1024))
+    units = pooled[...].astype(F32).reshape(128, 1024)
+    for copy in unit_copies:
+        copy.wait()
+    un = norm(units)
     tq = nt(un, tqt[0]).astype(BF16)
     tk = nt(un, tqt[1]).astype(BF16)
     tvt = nt(tqt[2], un).astype(BF16)
@@ -317,9 +343,8 @@
     e = jnp.exp2((st - jnp.max(st, axis=0, keepdims=True)) * EXP_SCALE)
     tat[me] = (nn(tvt, e.astype(BF16)) / jnp.sum(e, axis=0, keepdims=True)).astype(BF16)
     cast_start(1, tat)
-    hop(1 + CO, 1)
-    hop(1 + TO, 2)
-    lag(1 + TO, 1)
+    hop(1 + CO, 4)
+    lag(1 + CO, 3)
     settle(1 + CQ)
 
     def put_query(n, cols, o):
@@ -328,19 +353,10 @@
         cq[2 * n + 1] = o[:, 128:]
 
     square(xr, CQ, put_query)
-    hop(1 + TO, 3)
-    lag(1 + TO, 2)
-    hop(1 + CO, 2)
-    lag(1 + CO, 1)
-    hop(1 + TO, 4)
-    lag(1 + TO, 3)
+    lag(1 + CO, 4)
     cast_finish(1, tat)
-    hop(1 + CO, 3)
-    lag(1 + CO, 2)
-    lag(1 + TO, 4)
     settle(1 + TO)
 
-    units = pooled[...].reshape(128, 1024)
     chips = []
     for s in range(8):
         off = (s + 1) // 2 * (1 - 2 * (s % 2))
@@ -352,9 +368,7 @@
     ckv[me, 0] = nt(ckt[0], up).astype(BF16)
     ckv[me, 1] = nt(ckt[1], up).astype(BF16)
     cast_start(2, ckv)
-    hop(1 + CO, 4)
-    lag(1 + CO, 3)
-    lag(1 + CO, 4)
+    settle(1 + CO)
     cast_finish(2, ckv)
 
     def cross(p, _):
@@ -370,8 +384,6 @@
         return 0
 
     lax.fori_loop(0, 8, cross, 0)
-
-    settle(1 + CO)
 
     def put_out(n, cols, o):
         out[:, cols] = (lt[:, cols].astype(F32) + o).astype(BF16)
@@ -403,7 +415,7 @@
     return pl.pallas_call(
         kernel,
         out_shape=jax.ShapeDtypeStruct((256, 1024), BF16),
-        in_specs=[pl.BlockSpec(memory_space=pltpu.VMEM)] * 8,
+        in_specs=[pl.BlockSpec(memory_space=pltpu.VMEM)] + [pl.BlockSpec(memory_space=pl.ANY)] * 7,
         out_specs=pl.BlockSpec(memory_space=pltpu.VMEM),
         scratch_shapes=[
             pltpu.VMEM((16, 64, 3072), BF16),
@@ -415,7 +427,7 @@
             pltpu.VMEM((2, 128, 640), F32),
             pltpu.VMEM((8, 256, 128), BF16),
             pltpu.VMEM((256, 1024), BF16),
-            pltpu.VMEM((16, 8, 1024), F32),
+            pltpu.VMEM((16, 8, 1024), BF16),
             pltpu.VMEM((16, 64, 128), BF16),
             pltpu.VMEM((16, 2, 64, 128), BF16),
             pltpu.VMEM((8, 256, 128), BF16),
@@ -426,6 +438,7 @@
             dma((8,)), dma((8,)),
             dma((3, 8)), dma((3, 8)), dma((3, 8)), dma((3, 8)),
             dma((5, 16)), dma((5, 16)), dma, dma,
+            pltpu.VMEM((3, 64, 1024), BF16), pltpu.VMEM((2, 64, 1024), BF16), dma((2,)),
         ],
         compiler_params=pltpu.CompilerParams(
             collective_id=0, has_side_effects=True, vmem_limit_bytes=60 * 1024 * 1024

time: 115 us -> 105 us (0.913)
  Pallas kernels: 113 us -> 102 us
    pallas_call x1, Pallas kernels: 113 us -> 102 us  [local(): pl.pallas_call(kernel, out_shape=jax.ShapeDtypeStruct((256, 1024), BF16),...]
where the time goes in v3:
time: 105 us; the launch traced here: 104 us
  Pallas kernels  102 us (97%)
  local copies, waits for them, and re-layouts  1.87 us (2%)
    pallas_call x1, Pallas kernels, local(): pl.pallas_call(kernel, out_shape=jax.ShapeDtypeStruct((256, 1024), BF16),...  102 us

profile of v3, /device:TPU:1, one launch (start us, length us, event | category | flops | bytes accessed | tf_op | source)
XLA Modules:
  0.0 104.4 jit_solution(5761900489337655112)
XLA Ops:
  0.0 102.5 %layer.1 = bf16[256,1024]{1,0:T(8,128)(2,1)} custom-call(bf16[256,1024]{1,0:T(8,128)(2,1)} %tok.1, bf16[64,3072]{1,0:T(8,128)(2,1)} %w_qkv.1, bf16[64,1024]{1,0:T(8,128)(2,1)} %w_bo.1, bf16[64,1024]{1,0:T(8,128)(2,1)} %w_cq.1, bf16[64,1024]{1,0:T(8,128)(2,1)} %w_to.1, bf16[64,1024]{1,0:T(8,128)(2,1)} %w_co.1, bf16[3,64,1024]{2,1,0:T(8,128)(2,1)} %bitcast.2, ...), custom_call_target="tpu_custom_call" | custom-call | tf_op jit(solution)/shard_map/layer/pallas_call | solution.py:415
  102.5 1.9 %copy.10 = bf16[256,1024]{1,0:T(8,128)(2,1)} copy(bf16[256,1024]{1,0:T(8,128)(2,1)} %layer.1) | data formatting | bytes 1048576

commit v4 on v3

--- a/solution.py
+++ b/solution.py
@@ -30,10 +30,10 @@
 
 
 def kernel(
-    tok, w_qkv, w_bo, w_cq, w_to, w_co, tq_hbm, ck_hbm, out,
+    tok_hbm, w_qkv, w_bo, w_cq, w_to, w_co, tq_hbm, ck_hbm, out,
     wq, w2, xr, acc, qb, kv, bias, at, lt, pooled, tat, ckv, cq, tokh, xh, acch,
     ring_s, ring_r, par_s, par_r, own_s, halo_s, halo_r, cast_s, cast_r, fwd_s, fwd_r,
-    side_s, side_r, tok_s, tok_r, tqt, ckt, unit_s,
+    side_s, side_r, tok_s, tok_r, tqt, ckt, unit_s, tok, out_v, out_s,
 ):
     me = lax.axis_index("seq")
     z, c = me // 2, me % 2
@@ -59,6 +59,8 @@
             device_id={"seq": to}, device_id_type=MESH,
         )
 
+    tok_in = pltpu.make_async_copy(tok_hbm, tok, unit_s.at[2])
+    tok_in.start()
     unit_copies = (
         pltpu.make_async_copy(tq_hbm, tqt, unit_s.at[0]),
         pltpu.make_async_copy(ck_hbm, ckt, unit_s.at[1]),
@@ -148,9 +150,10 @@
             have(w, s)
 
     launch(0)
-    tok_copy = remote(tok, tokh, tok_s, tok_r, far)
+    tok_copy = remote(tok_hbm, tokh, tok_s, tok_r, far)
     tok_copy.start()
 
+    tok_in.wait()
     xn = norm(tok[...].astype(F32))
     for p in range(8):
         xr[slot_of(p)] = xn[:, 128 * p : 128 * p + 128]
@@ -386,10 +389,14 @@
     lax.fori_loop(0, 8, cross, 0)
 
     def put_out(n, cols, o):
-        out[:, cols] = (lt[:, cols].astype(F32) + o).astype(BF16)
+        out_v[n] = (lt[:, cols].astype(F32) + o).astype(BF16)
+        pltpu.make_async_copy(out_v.at[n], out.at[:, cols], out_s.at[n]).start()
 
     square(at, CO, put_out)
 
+    for n in range(4):
+        cols = pl.ds(256 * n, 256)
+        pltpu.make_async_copy(out_v.at[n], out.at[:, cols], out_s.at[n]).wait()
     for w in range(5):
         par_copy(w, 0, 0).wait_send()
         for h in range(1, 5):
@@ -415,8 +422,8 @@
     return pl.pallas_call(
         kernel,
         out_shape=jax.ShapeDtypeStruct((256, 1024), BF16),
-        in_specs=[pl.BlockSpec(memory_space=pltpu.VMEM)] + [pl.BlockSpec(memory_space=pl.ANY)] * 7,
-        out_specs=pl.BlockSpec(memory_space=pltpu.VMEM),
+        in_specs=[pl.BlockSpec(memory_space=pl.ANY)] * 8,
+        out_specs=pl.BlockSpec(memory_space=pl.ANY),
         scratch_shapes=[
             pltpu.VMEM((16, 64, 3072), BF16),
             pltpu.VMEM((4, 16, 64, 1024), BF16),
@@ -438,7 +445,8 @@
             dma((8,)), dma((8,)),
             dma((3, 8)), dma((3, 8)), dma((3, 8)), dma((3, 8)),
             dma((5, 16)), dma((5, 16)), dma, dma,
-            pltpu.VMEM((3, 64, 1024), BF16), pltpu.VMEM((2, 64, 1024), BF16), dma((2,)),
+            pltpu.VMEM((3, 64, 1024), BF16), pltpu.VMEM((2, 64, 1024), BF16), dma((3,)),
+            pltpu.VMEM((256, 1024), BF16), pltpu.VMEM((4, 256, 256), BF16), dma((4,)),
         ],
         compiler_params=pltpu.CompilerParams(
             collective_id=0, has_side_effects=True, vmem_limit_bytes=60 * 1024 * 1024

time: 105 us -> 103 us (0.981)
    pallas_call x1, Pallas kernels: 102 us -> 101 us  [local(): pl.pallas_call(kernel, out_shape=jax.ShapeDtypeStruct((256, 1024), BF16),...]
where the time goes in v4:
time: 103 us
  Pallas kernels  101 us (98%)
  local copies, waits for them, and re-layouts  1.87 us (2%)
    pallas_call x1, Pallas kernels, local(): pl.pallas_call(kernel, out_shape=jax.ShapeDtypeStruct((256, 1024), BF16),...  101 us

profile of v4, /device:TPU:1, one launch (start us, length us, event | category | flops | bytes accessed | tf_op | source)
XLA Modules:
  0.0 102.7 jit_solution(4255244227317919927)
XLA Ops:
  0.0 100.8 %layer.1 = bf16[256,1024]{1,0:T(8,128)(2,1)} custom-call(bf16[256,1024]{1,0:T(8,128)(2,1)} %tok_hbm.1, bf16[64,3072]{1,0:T(8,128)(2,1)} %w_qkv.1, bf16[64,1024]{1,0:T(8,128)(2,1)} %w_bo.1, bf16[64,1024]{1,0:T(8,128)(2,1)} %w_cq.1, bf16[64,1024]{1,0:T(8,128)(2,1)} %w_to.1, bf16[64,1024]{1,0:T(8,128)(2,1)} %w_co.1, bf16[3,64,1024]{2,1,0:T(8,128)(2,1)} %bitcast.2, ...), custom_call_target="tpu_custom_call" | custom-call | tf_op jit(solution)/shard_map/layer/pallas_call | solution.py:422
  100.8 1.9 %copy.10 = bf16[256,1024]{1,0:T(8,128)(2,1)} copy(bf16[256,1024]{1,0:T(8,128)(2,1)} %layer.1) | data formatting | bytes 1048576
